TPU v7x, 32 devices: a whole 2x2x4 slice. The times are simulated.
32 devices in a mesh: dp: 2 (over core), ctx: 4 (over z), tensor: 4 (over y, x).
Axes of the slice: x: 2, y: 2, z: 4, core: 2. Of those that a mesh axis runs over, the one named last changes fastest.
Arguments:
- tokens: bfloat16 [4096, 2048], P(('dp', 'ctx')), may hold values from -6 to 6
- lengths: int32 [2, 13], P('dp'), may hold values from 1 to 819, 2048 in all within a row
- parents: int32 [2, 13], P('dp'), may hold values from 0 to 4, as said below
- w_query: bfloat16 [2048, 2048], P(('dp', 'ctx'), 'tensor'), may hold values from -0.125 to 0.125
- w_key: bfloat16 [2048, 1024], P(('dp', 'ctx'), 'tensor'), may hold values from -0.125 to 0.125
- w_value: bfloat16 [2048, 1024], P(('dp', 'ctx'), 'tensor'), may hold values from -0.125 to 0.125
- w_out: bfloat16 [2048, 2048], P('tensor', ('dp', 'ctx')), may hold values from -1.5 to 1.5
- w_gate: bfloat16 [2048, 6144], P(('dp', 'ctx'), 'tensor'), may hold values from -0.125 to 0.125
- w_up: bfloat16 [2048, 6144], P(('dp', 'ctx'), 'tensor'), may hold values from -0.125 to 0.125
- w_down: bfloat16 [6144, 2048], P('tensor', ('dp', 'ctx')), may hold values from -0.078125 to 0.078125
- gain_attn: bfloat16 [2048], P(('dp', 'ctx')), may hold values from 0.099609375 to 1.8984375
- gain_mlp: bfloat16 [2048], P(('dp', 'ctx')), may hold values from 0.099609375 to 1.8984375
- gain_query: bfloat16 [128], P(('dp', 'ctx')), may hold values from 0.099609375 to 1.8984375
- gain_key: bfloat16 [128], P(('dp', 'ctx')), may hold values from 0.099609375 to 1.8984375
- cotangent: bfloat16 [4096, 2048], P(('dp', 'ctx')), may hold values from -6 to 6
Outputs:
- result: bfloat16 [4096, 2048], P(('dp', 'ctx'))
- grad_tokens: float32 [4096, 2048], P(('dp', 'ctx'))
- grad_query: float32 [2048, 2048], P(('dp', 'ctx'), 'tensor')
- grad_key: float32 [2048, 1024], P(('dp', 'ctx'), 'tensor')
- grad_value: float32 [2048, 1024], P(('dp', 'ctx'), 'tensor')
- grad_out: float32 [2048, 2048], P('tensor', ('dp', 'ctx'))
- grad_gate: float32 [2048, 6144], P(('dp', 'ctx'), 'tensor')
- grad_up: float32 [2048, 6144], P(('dp', 'ctx'), 'tensor')
- grad_down: float32 [6144, 2048], P('tensor', ('dp', 'ctx'))
- grad_gain_attn: float32 [2048], P(('dp', 'ctx'))
- grad_gain_mlp: float32 [2048], P(('dp', 'ctx'))
- grad_gain_query: float32 [128], P(('dp', 'ctx'))
- grad_gain_key: float32 [128], P(('dp', 'ctx'))
Inputs may be any that keep to these rules, and one draw needn't show every extreme that they name: lengths[t, s] counts the tokens of segment s of tree t; the segments lie in order and each tree's lengths sum to 2048. parents[t, s] is the segment from which segment s of tree t hangs; segments 0 to 4 name 0 (segment 0 is the root), segments 5 to 12 name one of 1 to 4.
All inputs are finite; a program needn't handle non-finite values.
Results may differ from a plain program's by a relative error of at most 0.02.
Values may be sent and summed in bfloat16 or wider, within the bound.
No kernel may reach another device: no remote copies, remote signals or barrier semaphores. Data moves between devices by JAX's collectives and lax.ppermute only.
A program may use at most 192 MiB of HBM per device.

v0:
```python
import math

import jax
import jax.numpy as jnp
from jax import lax
from jax.sharding import PartitionSpec as P

HEAD_DIM = 128


EPS = 1e-06
THETA = 1000000.0
PRECISE = lax.Precision.HIGHEST


def norm_rows(values, gain_vec):
    scales = lax.rsqrt(jnp.mean(values * values, axis=-1, keepdims=True) + EPS)
    return (values * scales * gain_vec, scales)


def norm_back(grad_in, values, gain_vec, scales):
    upstream = grad_in * gain_vec
    inner_mean = jnp.mean(upstream * values, axis=-1, keepdims=True)
    return (
        scales * upstream - values * scales * scales * scales * inner_mean,
        grad_in * values * scales,
    )


def rotate_pairs(values, cosine, sine_vals):
    half_dim = values.shape[-1] // 2
    first_half = values[..., :half_dim]
    second_half = values[..., half_dim:]
    return jnp.concatenate(
        [
            first_half * cosine - second_half * sine_vals,
            second_half * cosine + first_half * sine_vals,
        ],
        axis=-1,
    )


def rotate_back(values, cosine, sine_vals):
    half_dim = values.shape[-1] // 2
    first_half = values[..., :half_dim]
    second_half = values[..., half_dim:]
    return jnp.concatenate(
        [
            first_half * cosine + second_half * sine_vals,
            second_half * cosine - first_half * sine_vals,
        ],
        axis=-1,
    )


def inner_rows(left, right):
    return lax.dot_general(
        left, right, (((0,), (0,)), ((), ())), preferred_element_type=jnp.float32
    )


def outer_cols(left, right):
    return lax.dot_general(
        left, right, (((1,), (1,)), ((), ())), preferred_element_type=jnp.float32
    )


def tensor_sum(values):
    return lax.psum(values, "tensor")


def tree_layout(lengths, parents, tree_total):
    seg_count = lengths.shape[0]
    index = jnp.arange(seg_count, dtype=jnp.int32)
    direct = ((parents[:, None] == index[None, :]) & (parents[:, None] != index[:, None])).astype(
        jnp.float32
    )
    reach = direct
    for closure_step in range(4):
        reach = jnp.minimum(reach + jnp.dot(reach, reach, precision=PRECISE), 1.0)
    ends = jnp.cumsum(lengths, dtype=jnp.int32)
    starts = ends - lengths
    offset = jnp.dot(reach, lengths.astype(jnp.float32), precision=PRECISE)
    places = jnp.arange(tree_total, dtype=jnp.int32)
    member = (starts[None, :] <= places[:, None]).astype(jnp.int32)
    segment_ids = jnp.sum(member, axis=1, dtype=jnp.int32) - 1
    onehot = (segment_ids[:, None] == index[None, :]).astype(jnp.float32)
    base = jnp.dot(onehot, offset - starts.astype(jnp.float32), precision=PRECISE)
    position = places.astype(jnp.float32) + base
    return (segment_ids, onehot, reach, position)


def on_device(
    tokens,
    lengths,
    parents,
    w_query,
    w_key,
    w_value,
    w_out,
    w_gate,
    w_up,
    w_down,
    gain_attn,
    gain_mlp,
    gain_query,
    gain_key,
    cotangent,
):
    row_count = tokens.shape[0]
    tree_total = row_count * lax.axis_size("ctx")
    start_row = lax.axis_index("ctx") * row_count
    attn_set = (
        lax.all_gather(w_query, ("dp", "ctx"), axis=0, tiled=True),
        lax.all_gather(w_key, ("dp", "ctx"), axis=0, tiled=True),
        lax.all_gather(w_value, ("dp", "ctx"), axis=0, tiled=True),
        lax.all_gather(w_out, ("dp", "ctx"), axis=1, tiled=True),
        lax.all_gather(gain_attn, ("dp", "ctx"), axis=0, tiled=True),
        lax.all_gather(gain_query, ("dp", "ctx"), axis=0, tiled=True),
        lax.all_gather(gain_key, ("dp", "ctx"), axis=0, tiled=True),
    )
    mlp_set = (
        lax.all_gather(w_gate, ("dp", "ctx"), axis=0, tiled=True),
        lax.all_gather(w_up, ("dp", "ctx"), axis=0, tiled=True),
        lax.all_gather(w_down, ("dp", "ctx"), axis=1, tiled=True),
        lax.all_gather(gain_mlp, ("dp", "ctx"), axis=0, tiled=True),
    )
    wq_full, wk_full, wv_full, wo_full, gain_one, gain_q, gain_k = attn_set
    wg_full, wu_full, wd_full, gain_two = mlp_set
    segment_all, onehot_all, reach, position_all = tree_layout(lengths[0], parents[0], tree_total)
    segment_here = lax.dynamic_slice_in_dim(segment_all, start_row, row_count)
    onehot_here = lax.dynamic_slice_in_dim(onehot_all, start_row, row_count)
    position = lax.dynamic_slice_in_dim(position_all, start_row, row_count)
    place_here = start_row + jnp.arange(row_count, dtype=jnp.int32)
    place_all = jnp.arange(tree_total, dtype=jnp.int32)
    ancestor = (
        jnp.dot(jnp.dot(onehot_here, reach, precision=PRECISE), onehot_all.T, precision=PRECISE)
        > 0.5
    )
    allowed = (segment_here[:, None] == segment_all[None, :]) & (
        place_all[None, :] <= place_here[:, None]
    ) | ancestor
    half_dim = HEAD_DIM // 2
    frequency = jnp.exp(
        jnp.arange(half_dim, dtype=jnp.float32) * (-2.0 * math.log(THETA) / HEAD_DIM)
    )
    angles = position[:, None] * frequency[None, :]
    cosine = jnp.cos(angles)[:, None, :]
    sine_vals = jnp.sin(angles)[:, None, :]
    score_scale = 1.0 / math.sqrt(HEAD_DIM)
    inputs = tokens.astype(jnp.float32)
    gain_onef = gain_one.astype(jnp.float32)
    normed_f, scale_one = norm_rows(inputs, gain_onef)
    normed_attn = normed_f.astype(jnp.bfloat16)
    q_raw = jnp.dot(normed_attn, wq_full, preferred_element_type=jnp.float32)
    k_raw = jnp.dot(normed_attn, wk_full, preferred_element_type=jnp.float32)
    v_bf = jnp.dot(normed_attn, wv_full, preferred_element_type=jnp.float32).astype(jnp.bfloat16)
    heads_here = q_raw.shape[1] // HEAD_DIM
    kv_here = k_raw.shape[1] // HEAD_DIM
    group_size = heads_here // kv_here
    gain_qf = gain_q.astype(jnp.float32)
    gain_kf = gain_k.astype(jnp.float32)
    q_heads = q_raw.reshape(row_count, heads_here, HEAD_DIM)
    k_heads = k_raw.reshape(row_count, kv_here, HEAD_DIM)
    q_normed, q_scales = norm_rows(q_heads, gain_qf)
    k_normed, k_scales = norm_rows(k_heads, gain_kf)
    q_bf = rotate_pairs(q_normed, cosine, sine_vals).astype(jnp.bfloat16)
    k_bf = rotate_pairs(k_normed, cosine, sine_vals).astype(jnp.bfloat16)
    k_all, v_all = (
        lax.all_gather(k_bf.reshape(row_count, kv_here * HEAD_DIM), "ctx", axis=0, tiled=True),
        lax.all_gather(v_bf, "ctx", axis=0, tiled=True),
    )
    k_all = k_all.reshape(tree_total, kv_here, HEAD_DIM)
    v_all = v_all.reshape(tree_total, kv_here, HEAD_DIM)
    q_grouped = q_bf.reshape(row_count, kv_here, group_size, HEAD_DIM)
    scores = (
        jnp.einsum("tkgd,skd->kgts", q_grouped, k_all, preferred_element_type=jnp.float32)
        * score_scale
    )
    scores = jnp.where(allowed[None, None], scores, -1e30)
    row_max = jnp.max(scores, axis=-1, keepdims=True)
    weights = jnp.exp(scores - row_max)
    prob_all = weights / jnp.sum(weights, axis=-1, keepdims=True)
    prob_bf = prob_all.astype(jnp.bfloat16)
    mixture = jnp.einsum("kgts,skd->tkgd", prob_bf, v_all, preferred_element_type=jnp.float32)
    mixture_bf = mixture.reshape(row_count, heads_here * HEAD_DIM).astype(jnp.bfloat16)
    attn_term = jnp.dot(mixture_bf, wo_full, preferred_element_type=jnp.float32)
    gain_twof = gain_two.astype(jnp.float32)
    hidden = inputs + tensor_sum(attn_term)
    normed_g, scale_two = norm_rows(hidden, gain_twof)
    normed_mlp = normed_g.astype(jnp.bfloat16)
    gate_pre = jnp.dot(normed_mlp, wg_full, preferred_element_type=jnp.float32)
    up_pre = jnp.dot(normed_mlp, wu_full, preferred_element_type=jnp.float32)
    gate_sig = jax.nn.sigmoid(gate_pre)
    gate_act = gate_pre * gate_sig
    inner_bf = (gate_act * up_pre).astype(jnp.bfloat16)
    mlp_term = jnp.dot(inner_bf, wd_full, preferred_element_type=jnp.float32)
    result = (hidden + tensor_sum(mlp_term)).astype(jnp.bfloat16)
    grad_result = cotangent.astype(jnp.float32)
    grad_down = inner_rows(inner_bf, cotangent)
    grad_inner = outer_cols(cotangent, wd_full)
    grad_gate_pre = (grad_inner * up_pre * gate_sig * (1.0 + gate_pre * (1.0 - gate_sig))).astype(
        jnp.bfloat16
    )
    grad_up_pre = (grad_inner * gate_act).astype(jnp.bfloat16)
    grad_gate = inner_rows(normed_mlp, grad_gate_pre)
    grad_up = inner_rows(normed_mlp, grad_up_pre)
    mlp_back_term = outer_cols(grad_gate_pre, wg_full) + outer_cols(grad_up_pre, wu_full)
    grad_normed_mlp = tensor_sum(mlp_back_term)
    grad_hidden_norm, gain_two_terms = norm_back(grad_normed_mlp, hidden, gain_twof, scale_two)
    grad_gain_mlp = jnp.sum(gain_two_terms, axis=0)
    grad_hidden = grad_result + grad_hidden_norm
    grad_attn_bf = grad_hidden.astype(jnp.bfloat16)
    grad_out = inner_rows(mixture_bf, grad_attn_bf)
    grad_mixture = (
        outer_cols(grad_attn_bf, wo_full)
        .astype(jnp.bfloat16)
        .reshape(row_count, kv_here, group_size, HEAD_DIM)
    )
    grad_probs = jnp.einsum(
        "tkgd,skd->kgts", grad_mixture, v_all, preferred_element_type=jnp.float32
    )
    grad_v_all = jnp.einsum(
        "kgts,tkgd->skd", prob_bf, grad_mixture, preferred_element_type=jnp.float32
    )
    row_total = jnp.sum(prob_all * grad_probs, axis=-1, keepdims=True)
    grad_scores = (prob_all * (grad_probs - row_total)).astype(jnp.bfloat16)
    grad_q = (
        jnp.einsum("kgts,skd->tkgd", grad_scores, k_all, preferred_element_type=jnp.float32)
        * score_scale
    )
    grad_k_all = (
        jnp.einsum("kgts,tkgd->skd", grad_scores, q_grouped, preferred_element_type=jnp.float32)
        * score_scale
    )
    grad_k, grad_v = (
        lax.psum_scatter(
            grad_k_all.reshape(tree_total, kv_here * HEAD_DIM),
            "ctx",
            scatter_dimension=0,
            tiled=True,
        ),
        lax.psum_scatter(
            grad_v_all.reshape(tree_total, kv_here * HEAD_DIM),
            "ctx",
            scatter_dimension=0,
            tiled=True,
        ),
    )
    grad_q = (
        grad_q.reshape(row_count, heads_here, HEAD_DIM).astype(jnp.bfloat16).astype(jnp.float32)
    )
    grad_k = grad_k.reshape(row_count, kv_here, HEAD_DIM).astype(jnp.bfloat16).astype(jnp.float32)
    grad_v_bf = grad_v.astype(jnp.bfloat16)
    grad_q_heads, q_gain_terms = norm_back(
        rotate_back(grad_q, cosine, sine_vals), q_heads, gain_qf, q_scales
    )
    grad_k_heads, k_gain_terms = norm_back(
        rotate_back(grad_k, cosine, sine_vals), k_heads, gain_kf, k_scales
    )
    grad_q_raw = grad_q_heads.reshape(row_count, heads_here * HEAD_DIM).astype(jnp.bfloat16)
    grad_k_raw = grad_k_heads.reshape(row_count, kv_here * HEAD_DIM).astype(jnp.bfloat16)
    grad_query = inner_rows(normed_attn, grad_q_raw)
    grad_key = inner_rows(normed_attn, grad_k_raw)
    grad_value = inner_rows(normed_attn, grad_v_bf)
    partial_value = (
        outer_cols(grad_q_raw, wq_full)
        + outer_cols(grad_k_raw, wk_full)
        + outer_cols(grad_v_bf, wv_full)
    )
    q_gain_part = jnp.sum(q_gain_terms, axis=(0, 1))
    k_gain_part = jnp.sum(k_gain_terms, axis=(0, 1))
    grad_normed_attn, grad_gain_query, grad_gain_key = (
        lax.psum(partial_value.astype(jnp.bfloat16), "tensor").astype(jnp.float32),
        lax.psum(q_gain_part.astype(jnp.bfloat16), "tensor").astype(jnp.float32),
        lax.psum(k_gain_part.astype(jnp.bfloat16), "tensor").astype(jnp.float32),
    )
    grad_input_norm, gain_one_terms = norm_back(grad_normed_attn, inputs, gain_onef, scale_one)
    grad_tokens = grad_hidden + grad_input_norm
    grad_gain_attn = jnp.sum(gain_one_terms, axis=0)
    (
        grad_query,
        grad_key,
        grad_value,
        grad_out,
        grad_gate,
        grad_up,
        grad_down,
        grad_gain_attn,
        grad_gain_mlp,
        grad_gain_query,
        grad_gain_key,
    ) = (
        lax.psum_scatter(
            grad_query.astype(jnp.bfloat16), ("dp", "ctx"), scatter_dimension=0, tiled=True
        ).astype(jnp.float32),
        lax.psum_scatter(
            grad_key.astype(jnp.bfloat16), ("dp", "ctx"), scatter_dimension=0, tiled=True
        ).astype(jnp.float32),
        lax.psum_scatter(
            grad_value.astype(jnp.bfloat16), ("dp", "ctx"), scatter_dimension=0, tiled=True
        ).astype(jnp.float32),
        lax.psum_scatter(
            grad_out.astype(jnp.bfloat16), ("dp", "ctx"), scatter_dimension=1, tiled=True
        ).astype(jnp.float32),
        lax.psum_scatter(
            grad_gate.astype(jnp.bfloat16), ("dp", "ctx"), scatter_dimension=0, tiled=True
        ).astype(jnp.float32),
        lax.psum_scatter(
            grad_up.astype(jnp.bfloat16), ("dp", "ctx"), scatter_dimension=0, tiled=True
        ).astype(jnp.float32),
        lax.psum_scatter(
            grad_down.astype(jnp.bfloat16), ("dp", "ctx"), scatter_dimension=1, tiled=True
        ).astype(jnp.float32),
        lax.psum_scatter(
            grad_gain_attn.astype(jnp.bfloat16), ("dp", "ctx"), scatter_dimension=0, tiled=True
        ).astype(jnp.float32),
        lax.psum_scatter(
            grad_gain_mlp.astype(jnp.bfloat16), ("dp", "ctx"), scatter_dimension=0, tiled=True
        ).astype(jnp.float32),
        lax.psum_scatter(
            grad_gain_query.astype(jnp.bfloat16), ("dp", "ctx"), scatter_dimension=0, tiled=True
        ).astype(jnp.float32),
        lax.psum_scatter(
            grad_gain_key.astype(jnp.bfloat16), ("dp", "ctx"), scatter_dimension=0, tiled=True
        ).astype(jnp.float32),
    )
    return (
        result,
        grad_tokens,
        grad_query,
        grad_key,
        grad_value,
        grad_out,
        grad_gate,
        grad_up,
        grad_down,
        grad_gain_attn,
        grad_gain_mlp,
        grad_gain_query,
        grad_gain_key,
    )


def solution(mesh):
    placed = (
        P(("dp", "ctx"), None),
        P("dp", None),
        P("dp", None),
        P(("dp", "ctx"), "tensor"),
        P(("dp", "ctx"), "tensor"),
        P(("dp", "ctx"), "tensor"),
        P("tensor", ("dp", "ctx")),
        P(("dp", "ctx"), "tensor"),
        P(("dp", "ctx"), "tensor"),
        P("tensor", ("dp", "ctx")),
        P(("dp", "ctx")),
        P(("dp", "ctx")),
        P(("dp", "ctx")),
        P(("dp", "ctx")),
        P(("dp", "ctx"), None),
    )
    return jax.shard_map(
        on_device,
        mesh=mesh,
        in_specs=placed,
        out_specs=(
            P(("dp", "ctx"), None),
            P(("dp", "ctx"), None),
            P(("dp", "ctx"), "tensor"),
            P(("dp", "ctx"), "tensor"),
            P(("dp", "ctx"), "tensor"),
            P("tensor", ("dp", "ctx")),
            P(("dp", "ctx"), "tensor"),
            P(("dp", "ctx"), "tensor"),
            P("tensor", ("dp", "ctx")),
            P(("dp", "ctx")),
            P(("dp", "ctx")),
            P(("dp", "ctx")),
            P(("dp", "ctx")),
        ),
        check_vma=False,
    )
```

profile of v0, /device:TPU:0, one launch (start us, length us, event | category | flops | bytes accessed | tf_op | source)
XLA Modules:
  0.0 1460.9 jit_solution(8026323037325675424)
XLA Ops:
  9.4 17.9 %all-gather = bf16[8,1,256]{2,1,0:T(2,128)(2,1)S(1)} all-gather(bf16[1,1,256]{2,1,0:T(2,128)(2,1)S(1)} %reshape.243), channel_id=1, replica_groups=mesh['dp'=2,'ctx'=4,'tensor'=4] {'dp','ctx'}, dimensions={0}, use_global_device_ids=true | all-gather | bytes 4608 | tf_op jit(solution)/shard_map/all_gather | solution.py:118
  29.6 4.9 all-gather.12.cloned.1.call-done
  34.6 3.3 convolution_convert_fusion.8
  40.3 16.3 %all-reduce.8 = (bf16[128]{0:T(256)(128)(2,1)S(1)}, bf16[128]{0:T(256)(128)(2,1)S(1)}) all-reduce(bf16[128]{0:T(256)(128)(2,1)S(1)} %dynamic-update-slice, bf16[128]{0:T(256)(128)(2,1)S(1)} %dynamic-update-slice.1), channel_id=1, replica_groups=mesh['dp'=2,'ctx'=4,'tensor'=4] {'dp','ctx'}, use_global_device_ids=true, to_apply=%add | all-reduce | flops 256 | bytes 1024
  64.4 3.2 fusion.25
  70.3 17.6 %all-gather.14.cloned.1.call-done = bf16[2048,256]{1,0:T(8,128)(2,1)} async-done(((bf16[512,256]{1,0:T(8,128)(2,1)}), bf16[2048,256]{1,0:T(8,128)(2,1)}) %all-gather.14.cloned.1.call-update) | async-done | bytes 1048592 | tf_op jit(solution)/shard_map/all_gather | solution.py:171
  90.2 27.7 %all-gather.20.cloned.1.call-done = bf16[2048,512]{1,0:T(8,128)(2,1)} async-done(((bf16[256,512]{1,0:T(8,128)(2,1)}), bf16[2048,512]{1,0:T(8,128)(2,1)}) %all-gather.20.cloned.1.call-update) | async-done | bytes 2097168 | tf_op jit(solution)/shard_map/all_gather | solution.py:114
  122.8 24.4 %all-gather.18.cloned.1.call-done = bf16[2048,256]{0,1:T(8,128)(2,1)} async-done(((bf16[512,256]{0,1:T(8,128)(2,1)}), bf16[2048,256]{0,1:T(8,128)(2,1)}) %all-gather.18.cloned.1.call-update) | async-done | bytes 1048592 | tf_op jit(solution)/shard_map/all_gather | solution.py:170
  147.3 13.9 fusion.81
  161.2 7.6 fusion.32
  168.8 9.9 all-gather.22.cloned.1.call-done
  178.7 4.9 fusion.82
  185.8 16.4 %all-gather.1 = bf16[8,1,256]{2,1,0:T(2,128)(2,1)S(1)} all-gather(bf16[1,1,256]{2,1,0:T(2,128)(2,1)S(1)} %reshape.245), channel_id=1, replica_groups=mesh['dp'=2,'ctx'=4,'tensor'=4] {'dp','ctx'}, dimensions={0}, use_global_device_ids=true | all-gather | bytes 4608 | tf_op jit(solution)/shard_map/all_gather | solution.py:126
  202.2 84.2 %all-reduce.14.cloned.1.call-done = f32[512,2048]{1,0:T(8,128)} async-done(((f32[512,2048]{1,0:T(8,128)}), f32[512,2048]{1,0:T(8,128)}) %all-reduce.14.cloned.1.call-update) | async-done | bytes 4194320 | tf_op jit(solution)/shard_map/psum | solution.py:69
  293.0 59.8 %all-gather.24.cloned.1.call-done = bf16[2048,1536]{1,0:T(8,128)(2,1)} async-done(((bf16[256,1536]{1,0:T(8,128)(2,1)}), bf16[2048,1536]{1,0:T(8,128)(2,1)}) %all-gather.24.cloned.1.call-update) | async-done | bytes 6291472 | tf_op jit(solution)/shard_map/all_gather | solution.py:123
  352.8 8.5 fusion.83
  361.3 56.5 %all-gather.26.cloned.1.call-done = bf16[2048,1536]{1,0:T(8,128)(2,1)} async-done(((bf16[256,1536]{1,0:T(8,128)(2,1)}), bf16[2048,1536]{1,0:T(8,128)(2,1)}) %all-gather.26.cloned.1.call-update) | async-done | bytes 6291472 | tf_op jit(solution)/shard_map/all_gather | solution.py:124
  417.7 8.5 fusion.84
  426.2 56.8 %all-gather.28.cloned.1.call-done = bf16[1536,2048]{1,0:T(8,128)(2,1)} async-done(((bf16[1536,256]{1,0:T(8,128)(2,1)}), bf16[1536,2048]{1,0:T(8,128)(2,1)}) %all-gather.28.cloned.1.call-update) | async-done | bytes 6291472 | tf_op jit(solution)/shard_map/all_gather | solution.py:125
  483.0 9.8 multiply_convert_fusion.1
  492.9 7.3 fusion.86
  500.2 4.9 fusion.85
  505.2 5.0 convolution_add_fusion
  510.3 170.3 %all-reduce.18.cloned.1.call-done = (f32[512,2048]{1,0:T(8,128)}, f32[512,2048]{1,0:T(8,128)}) async-done(((f32[512,2048]{1,0:T(8,128)}, f32[512,2048]{1,0:T(8,128)}), (f32[512,2048]{1,0:T(8,128)}, f32[512,2048]{1,0:T(8,128)})) %all-reduce.18.cloned.1.call-update) | async-done | bytes 8388624 | tf_op jit(solution)/shard_map/psum | solution.py:69
  680.6 4.7 multiply_reduce_fusion
  685.3 6.6 subtract_add_fusion
  696.3 9.5 fusion.1
  705.7 11.6 fusion.3
  717.3 3.9 fusion.27
  721.4 10.0 fusion.20
  731.7 5.1 fusion.31
  740.9 4.8 convolution_convert_fusion.3
  745.8 8.2 convolution_convert_fusion.2
  754.1 8.2 convolution_convert_fusion.1
  770.1 40.8 %reduce-scatter.12.cloned.1.call-done = f32[512,256]{0,1:T(8,128)} async-done(((f32[2048,256]{0,1:T(8,128)}), f32[512,256]{0,1:T(8,128)}) %reduce-scatter.12.cloned.1.call-update) | async-done | bytes 524304 | tf_op jit(solution)/shard_map/reduce_scatter | solution.py:243
  813.6 4.3 add_convert_fusion
  818.0 8.2 convolution_convert_fusion
  831.6 29.7 %reduce-scatter.14.cloned.1.call-done = bf16[256,512]{1,0:T(8,128)(2,1)} async-done(((bf16[2048,512]{1,0:T(8,128)(2,1)}), bf16[256,512]{1,0:T(8,128)(2,1)}) %reduce-scatter.14.cloned.1.call-update) | async-done | bytes 262160 | tf_op jit(solution)/shard_map/reduce_scatter | solution.py:294
  863.2 48.6 %reduce-scatter.20.cloned.1.call-done = bf16[512,256]{1,0:T(8,128)(2,1)} async-done(((bf16[512,2048]{1,0:T(8,128)(2,1)}), bf16[512,256]{1,0:T(8,128)(2,1)}) %reduce-scatter.20.cloned.1.call-update) | async-done | bytes 262160 | tf_op jit(solution)/shard_map/reduce_scatter | solution.py:303
  913.6 127.4 %reduce-scatter.22.cloned.1.call-done = bf16[256,1536]{1,0:T(8,128)(2,1)} async-done(((bf16[2048,1536]{1,0:T(8,128)(2,1)}), bf16[256,1536]{1,0:T(8,128)(2,1)}) %reduce-scatter.22.cloned.1.call-update) | async-done | bytes 786448 | tf_op jit(solution)/shard_map/reduce_scatter | solution.py:306
  1043.4 128.1 %reduce-scatter.24.cloned.1.call-done = bf16[256,1536]{1,0:T(8,128)(2,1)} async-done(((bf16[2048,1536]{1,0:T(8,128)(2,1)}), bf16[256,1536]{1,0:T(8,128)(2,1)}) %reduce-scatter.24.cloned.1.call-update) | async-done | bytes 786448 | tf_op jit(solution)/shard_map/reduce_scatter | solution.py:309
  1174.0 70.6 %all-reduce.16.cloned.1.call-done = bf16[512,2048]{1,0:T(8,128)(2,1)} async-done(((bf16[512,2048]{1,0:T(8,128)(2,1)}), bf16[512,2048]{1,0:T(8,128)(2,1)}) %all-reduce.16.cloned.1.call-update) | async-done | bytes 2097168 | tf_op jit(solution)/shard_map/psum | solution.py:274
  1247.7 20.1 %all-reduce.7 = (bf16[2048]{0:T(1024)(128)(2,1)S(1)}, bf16[2048]{0:T(1024)(128)(2,1)S(1)}, bf16[128]{0:T(256)(128)(2,1)S(1)}, bf16[128]{0:T(256)(128)(2,1)S(1)}) all-reduce(bf16[2048]{0:T(1024)(128)(2,1)S(1)} %get-tuple-element.15, ...), channel_id=11, replica_groups=mesh['dp'=2,'ctx'=4,'tensor'=4] {'dp','ctx'}, use_global_device_ids=true, to_apply=%region_27.28.clone | all-reduce | flops 4352 | bytes 17408
  1268.0 108.0 %reduce-scatter.26.cloned.1.call-done = bf16[1536,256]{1,0:T(8,128)(2,1)} async-done(((bf16[1536,2048]{1,0:T(8,128)(2,1)}), bf16[1536,256]{1,0:T(8,128)(2,1)}) %reduce-scatter.26.cloned.1.call-update) | async-done | bytes 786448 | tf_op jit(solution)/shard_map/reduce_scatter | solution.py:312
  1378.4 9.8 all-reduce.9
  1389.2 25.4 %reduce-scatter.16.cloned.1.call-done = bf16[256,256]{1,0:T(8,128)(2,1)} async-done(((bf16[2048,256]{1,0:T(8,128)(2,1)}), bf16[256,256]{1,0:T(8,128)(2,1)}) %reduce-scatter.16.cloned.1.call-update) | async-done | bytes 131088 | tf_op jit(solution)/shard_map/reduce_scatter | solution.py:297
  1416.8 6.3 fusion.15
  1423.2 28.8 %reduce-scatter.18.cloned.1.call-done = bf16[256,256]{1,0:T(8,128)(2,1)} async-done(((bf16[2048,256]{1,0:T(8,128)(2,1)}), bf16[256,256]{1,0:T(8,128)(2,1)}) %reduce-scatter.18.cloned.1.call-update) | async-done | bytes 131088 | tf_op jit(solution)/shard_map/reduce_scatter | solution.py:300
  (231 shorter events, 75.0 us)
Async XLA Ops:
  7.2 27.4 %all-gather.12.cloned.1.call-start = ((), (), s32[]{:S(2)}) async-start(), calls=%async_computation.9 | async-start | bytes 1179648 | tf_op jit(solution)/shard_map/all_gather | solution.py:116
  7.9 51.2 %all-gather.16.cloned.1.call-start = ((), (), s32[]{:S(2)}) async-start(), calls=%async_computation.11 | async-start | bytes 1179648 | tf_op jit(solution)/shard_map/all_gather | solution.py:115
  8.7 79.2 %all-gather.14.cloned.1.call-start = ((), (), s32[]{:S(2)}) async-start(), calls=%async_computation.10 | async-start | bytes 1310720 | tf_op jit(solution)/shard_map/all_gather | solution.py:171
  27.3 90.6 %copy-start.21 = (f32[8,1,256]{2,1,0:T(1,128)}, f32[8,1,256]{2,1,0:T(1,128)S(1)}, u32[]{:S(2)}) copy-start(f32[8,1,256]{2,1,0:T(1,128)S(1)} %convert_element_type.255) | copy-start | bytes 24580
  27.3 11.3 copy-start.33
  27.3 12.5 copy-start.35
  27.3 12.8 copy-start.36
  27.3 29.3 %copy-start.34 = (s32[1,13]{1,0:T(1,128)S(1)}, s32[1,13]{1,0:T(1,128)}, u32[]{:S(2)}) copy-start(s32[1,13]{1,0:T(1,128)} %param.16) | copy-start | bytes 160
  27.3 29.5 %copy-start.37 = (s32[1,13]{1,0:T(1,128)S(1)}, s32[1,13]{1,0:T(1,128)}, u32[]{:S(2)}) copy-start(s32[1,13]{1,0:T(1,128)} %param.17) | copy-start | bytes 160
  27.4 31.8 %copy-start.3 = (bf16[512,2048]{1,0:T(8,128)(2,1)S(1)}, bf16[512,2048]{1,0:T(8,128)(2,1)}, u32[]{:S(2)}) copy-start(bf16[512,2048]{1,0:T(8,128)(2,1)} %param.15) | copy-start | bytes 6291460
  29.6 88.3 %copy-start.27 = (f32[512]{0:T(512)}, f32[512]{0:T(512)S(1)}, u32[]{:S(2)}) copy-start(f32[512]{0:T(512)S(1)} %add_rsqrt_fusion.3) | copy-start | bytes 6148
  37.9 80.0 %all-gather.20.cloned.1.call-start = ((), (), s32[]{:S(2)}) async-start(), calls=%async_computation.13 | async-start | bytes 2359296 | tf_op jit(solution)/shard_map/all_gather | solution.py:114
  38.5 108.8 %all-gather.18.cloned.1.call-start = ((), (), s32[]{:S(2)}) async-start(), calls=%async_computation.12 | async-start | bytes 1310720 | tf_op jit(solution)/shard_map/all_gather | solution.py:170
  59.1 63.0 %copy-start.10 = (f32[512,64]{0,1:T(8,128)}, f32[512,64]{0,1:T(8,128)S(1)}, u32[]{:S(2)}) copy-start(f32[512,64]{0,1:T(8,128)S(1)} %get-tuple-element.50) | copy-start | bytes 393220
  59.1 63.0 %copy-start.12 = (f32[512,64]{0,1:T(8,128)}, f32[512,64]{0,1:T(8,128)S(1)}, u32[]{:S(2)}) copy-start(f32[512,64]{0,1:T(8,128)S(1)} %get-tuple-element.51) | copy-start | bytes 393220
  63.1 115.6 %all-gather.22.cloned.1.call-start = ((), (), s32[]{:S(2)}) async-start(), calls=%async_computation.14 | async-start | bytes 2359296 | tf_op jit(solution)/shard_map/all_gather | solution.py:117
  63.7 222.7 %all-reduce.14.cloned.1.call-start = ((), (), s32[]{:S(2)}) async-start(), calls=%async_computation.15 | async-start | bytes 8388608 | tf_op jit(solution)/shard_map/psum | solution.py:69
  64.2 56.7 %copy-start.29 = (f32[128]{0:T(128)}, f32[128]{0:T(128)S(1)}, u32[]{:S(2)}) copy-start(f32[128]{0:T(128)S(1)} %convert_element_type.203) | copy-start | bytes 1540
  122.8 38.3 %copy-start.14 = (bf16[512,4,64]{2,0,1:T(8,128)(2,1)}, bf16[512,4,64]{2,0,1:T(8,128)(2,1)S(1)}, u32[]{:S(2)}) copy-start(bf16[512,4,64]{2,0,1:T(8,128)(2,1)S(1)} %copy.66) | copy-start | bytes 786436
  168.8 14.8 %copy-start.18 = (bf16[2,128,2,512]{3,1,2,0:T(8,128)(2,1)}, bf16[2,128,2,512]{3,1,2,0:T(8,128)(2,1)S(1)}, u32[]{:S(2)}) copy-start(bf16[2,128,2,512]{3,1,2,0:T(8,128)(2,1)S(1)} %fusion.32) | copy-start | bytes 1572868
  183.7 169.1 %all-gather.24.cloned.1.call-start = ((), (), s32[]{:S(2)}) async-start(), calls=%async_computation.16 | async-start | bytes 7077888 | tf_op jit(solution)/shard_map/all_gather | solution.py:123
  184.4 233.3 %all-gather.26.cloned.1.call-start = ((), (), s32[]{:S(2)}) async-start(), calls=%async_computation.17 | async-start | bytes 7077888 | tf_op jit(solution)/shard_map/all_gather | solution.py:124
  185.1 297.8 %all-gather.28.cloned.1.call-start = ((), (), s32[]{:S(2)}) async-start(), calls=%async_computation.18 | async-start | bytes 7077888 | tf_op jit(solution)/shard_map/all_gather | solution.py:125
  185.7 494.9 %all-reduce.18.cloned.1.call-start = ((), (), s32[]{:S(2)}) async-start(), calls=%async_computation.29 | async-start | bytes 16777216 | tf_op jit(solution)/shard_map/psum | solution.py:69
  483.0 17.2 %slice-start.6 = ((s8[6291456]{0:T(1024)(128)(4,1)}), s8[4194304]{0:T(1024)(128)(4,1)S(1)}, s32[]{:S(2)}) async-start(s8[6291456]{0:T(1024)(128)(4,1)} %bitcast.248), calls=%async_computation.36 | async-start | bytes 8388608
  483.0 22.2 %slice-start.4 = ((s8[6291456]{0:T(1024)(128)(4,1)}), s8[2097152]{0:T(1024)(128)(4,1)S(1)}, s32[]{:S(2)}) async-start(s8[6291456]{0:T(1024)(128)(4,1)} %bitcast.246), calls=%async_computation.34 | async-start | bytes 4194304
  492.8 7.3 copy-start.42
  492.8 7.3 copy-start.41
  492.9 12.3 copy-start.40
  492.9 7.3 slice-start.7
  492.9 12.3 slice-start.5
  510.2 255.5 %reduce-scatter.10.cloned.1.call-start = ((), (), s32[]{:S(2)}) async-start(), calls=%async_computation.19 | async-start | bytes 2621440 | tf_op jit(solution)/shard_map/reduce_scatter | solution.py:237
  680.6 15.6 %slice-start = ((s8[16777216]{0:T(1024)(128)(4,1)}), s8[4194304]{0:T(1024)(128)(4,1)S(1)}, s32[]{:S(2)}) async-start(s8[16777216]{0:T(1024)(128)(4,1)} %bitcast.216), calls=%async_computation.30 | async-start | bytes 8388608
  685.3 8.8 copy-start.16
  685.3 10.8 slice-start.1
  685.3 10.8 slice-start.2
  685.3 11.0 slice-start.3
  705.7 11.6 copy-start.15
  721.3 10.4 copy-start.30
  721.3 89.6 %reduce-scatter.12.cloned.1.call-start = ((), (), s32[]{:S(2)}) async-start(), calls=%async_computation.20 | async-start | bytes 2621440 | tf_op jit(solution)/shard_map/reduce_scatter | solution.py:243
  731.4 130.0 %reduce-scatter.14.cloned.1.call-start = ((), (), s32[]{:S(2)}) async-start(), calls=%async_computation.22 | async-start | bytes 2359296 | tf_op jit(solution)/shard_map/reduce_scatter | solution.py:294
  740.9 170.9 %reduce-scatter.20.cloned.1.call-start = ((), (), s32[]{:S(2)}) async-start(), calls=%async_computation.25 | async-start | bytes 2359296 | tf_op jit(solution)/shard_map/reduce_scatter | solution.py:303
  745.8 295.2 %reduce-scatter.22.cloned.1.call-start = ((), (), s32[]{:S(2)}) async-start(), calls=%async_computation.26 | async-start | bytes 7077888 | tf_op jit(solution)/shard_map/reduce_scatter | solution.py:306
  754.1 417.5 %reduce-scatter.24.cloned.1.call-start = ((), (), s32[]{:S(2)}) async-start(), calls=%async_computation.27 | async-start | bytes 7077888 | tf_op jit(solution)/shard_map/reduce_scatter | solution.py:309
  762.3 482.3 %all-reduce.16.cloned.1.call-start = ((), (), s32[]{:S(2)}) async-start(), calls=%async_computation.21 | async-start | bytes 4194304 | tf_op jit(solution)/shard_map/psum | solution.py:274
  817.9 558.1 %reduce-scatter.26.cloned.1.call-start = ((), (), s32[]{:S(2)}) async-start(), calls=%async_computation.28 | async-start | bytes 7077888 | tf_op jit(solution)/shard_map/reduce_scatter | solution.py:312
  826.2 588.4 %reduce-scatter.16.cloned.1.call-start = ((), (), s32[]{:S(2)}) async-start(), calls=%async_computation.23 | async-start | bytes 1179648 | tf_op jit(solution)/shard_map/reduce_scatter | solution.py:297
  828.2 623.7 %reduce-scatter.18.cloned.1.call-start = ((), (), s32[]{:S(2)}) async-start(), calls=%async_computation.24 | async-start | bytes 1179648 | tf_op jit(solution)/shard_map/reduce_scatter | solution.py:300
  (24 other events, 69.1 us)
Sparse Core Ops, SparseCore 0:
  9.6 24.9 all-gather.11
  36.2 22.2 all-gather.15
  60.6 27.1 all-gather.13
  89.3 28.5 all-gather.19
  119.9 27.3 all-gather.17
  148.7 29.9 all-gather.21
  183.8 102.6 all-reduce.13
  288.0 64.6 all-gather.23
  354.4 63.3 all-gather.25
  419.2 63.7 all-gather.27
  510.3 170.2 all-reduce.17
  721.4 44.2 reduce-scatter.9
  768.0 42.8 reduce-scatter.11
  813.0 48.2 reduce-scatter.13
  863.5 48.2 reduce-scatter.19
  914.0 126.9 reduce-scatter.21
  1043.1 128.3 reduce-scatter.23
  1174.5 70.0 all-reduce.15
  1246.9 129.0 reduce-scatter.25
  1378.1 36.3 reduce-scatter.15
  1416.8 35.0 reduce-scatter.17
where the time goes:
time: 1470 us; the launch traced here: 1460 us
  waiting for transfers between devices  1130 us (77%)
  matrix products  160 us (11%)
  blocking collectives  80.5 us (5%)
  other arithmetic  60.2 us (4%)
  between operations  17.6 us (1%)
    psum x2, waiting for transfers between devices, tensor_sum(): return lax.psum(values, 'tensor')  255 us
    reduce_scatter x1, waiting for transfers between devices, on_device(): lax.psum_scatter(grad_up.astype(jnp.bfloat16), ('dp', 'ctx'), scatter_dim...  128 us
    reduce_scatter x1, waiting for transfers between devices, on_device(): lax.psum_scatter(grad_gate.astype(jnp.bfloat16), ('dp', 'ctx'), scatter_d...  127 us
    reduce_scatter x1, waiting for transfers between devices, on_device(): lax.psum_scatter(grad_down.astype(jnp.bfloat16), ('dp', 'ctx'), scatter_d...  108 us
    psum x1, waiting for transfers between devices, on_device(): lax.psum(partial_value.astype(jnp.bfloat16), 'tensor').astype(jnp.float32)  70.6 us
    all_gather x1, waiting for transfers between devices, on_device(): lax.all_gather(w_gate, ('dp', 'ctx'), axis=0, tiled=True)  59.8 us
    all_gather x1, waiting for transfers between devices, on_device(): lax.all_gather(w_down, ('dp', 'ctx'), axis=1, tiled=True)  56.8 us
    all_gather x1, waiting for transfers between devices, on_device(): lax.all_gather(w_up, ('dp', 'ctx'), axis=0, tiled=True)  56.5 us
  transfers between devices with their start and end apart: 21, of which 20 were waited for; matrix products, arithmetic and copies ran while one was open for 11% of the time, Pallas kernels for 0%

commit v1 on v0

v1 whole, which is shorter than its diff:
```python
import math

import jax
import jax.numpy as jnp
from jax import lax
from jax.sharding import PartitionSpec as P

HEAD_DIM = 128

EPS = 1e-06
THETA = 1000000.0
PRECISE = lax.Precision.HIGHEST
BF = jnp.bfloat16
F32 = jnp.float32
ROWS = ("dp", "ctx")


def row_scales(values):
    return lax.rsqrt(jnp.mean(values * values, axis=-1, keepdims=True) + EPS)


def norm_back(grad_in, values, gain_vec, scales):
    upstream = grad_in * gain_vec
    inner_mean = jnp.mean(upstream * values, axis=-1, keepdims=True)
    return (
        scales * upstream - values * scales * scales * scales * inner_mean,
        grad_in * values * scales,
    )


def rotate_pairs(values, cosine, sine_vals):
    half_dim = values.shape[-1] // 2
    first_half = values[..., :half_dim]
    second_half = values[..., half_dim:]
    return jnp.concatenate(
        [
            first_half * cosine - second_half * sine_vals,
            second_half * cosine + first_half * sine_vals,
        ],
        axis=-1,
    )


def rotate_back(values, cosine, sine_vals):
    return rotate_pairs(values, cosine, -sine_vals)


def dot(left, right):
    return jnp.dot(left, right, preferred_element_type=F32)


def inner_rows(left, right):
    return lax.dot_general(left, right, (((0,), (0,)), ((), ())), preferred_element_type=F32)


def outer_cols(left, right):
    return lax.dot_general(left, right, (((1,), (1,)), ((), ())), preferred_element_type=F32)


def swap(values, axis, mask):
    size = lax.axis_size(axis)
    return lax.ppermute(values, axis, [(a, a ^ mask) for a in range(size)])


def scatter_sum(partial):
    size = lax.axis_size("tensor")
    chunk = partial.shape[0] // size
    low = partial.astype(BF)
    total = partial[:chunk]
    for mask in range(1, size):
        total = total + swap(low[mask * chunk : (mask + 1) * chunk], "tensor", mask).astype(F32)
    return total


def gather_rows(own):
    size = lax.axis_size("tensor")
    return [own] + [swap(own, "tensor", mask) for mask in range(1, size)]


def xor_order(values):
    size = lax.axis_size("tensor")
    me = lax.axis_index("tensor")
    chunk = values.shape[0] // size
    return jnp.concatenate(
        [
            lax.dynamic_slice_in_dim(values, (me ^ mask) * chunk, chunk, axis=0)
            for mask in range(size)
        ],
        axis=0,
    )


def grad_scatter(left, right):
    half = left.shape[1] // 2
    me = lax.axis_index("dp")
    theirs = lax.dynamic_slice_in_dim(left, (1 - me) * half, half, axis=1)
    mine = lax.dynamic_slice_in_dim(left, me * half, half, axis=1)
    sent = swap(inner_rows(theirs, right).astype(BF), "dp", 1)
    both = (inner_rows(mine, right) + sent.astype(F32)).astype(BF)
    return lax.psum_scatter(both, "ctx", scatter_dimension=0, tiled=True)


def tree_layout(lengths, parents, tree_total):
    seg_count = lengths.shape[0]
    index = jnp.arange(seg_count, dtype=jnp.int32)
    direct = ((parents[:, None] == index[None, :]) & (parents[:, None] != index[:, None])).astype(
        F32
    )
    reach = direct
    for closure_step in range(4):
        reach = jnp.minimum(reach + jnp.dot(reach, reach, precision=PRECISE), 1.0)
    ends = jnp.cumsum(lengths, dtype=jnp.int32)
    starts = ends - lengths
    offset = jnp.dot(reach, lengths.astype(F32), precision=PRECISE)
    return starts, reach, offset


def segment_onehot(places, starts):
    index = jnp.arange(starts.shape[0], dtype=jnp.int32)
    member = (starts[None, :] <= places[:, None]).astype(jnp.int32)
    segment_ids = jnp.sum(member, axis=1, dtype=jnp.int32) - 1
    return segment_ids, (segment_ids[:, None] == index[None, :]).astype(F32)


def on_device(
    tokens,
    lengths,
    parents,
    w_query,
    w_key,
    w_value,
    w_out,
    w_gate,
    w_up,
    w_down,
    gain_attn,
    gain_mlp,
    gain_query,
    gain_key,
    cotangent,
):
    row_count, width = tokens.shape
    ctx_size = lax.axis_size("ctx")
    split = lax.axis_size("tensor")
    me_t = lax.axis_index("tensor")
    chunk = row_count // split
    tree_total = row_count * ctx_size
    q_cols, k_cols = w_query.shape[1], w_key.shape[1]

    w_qkv = lax.all_gather(
        jnp.concatenate([w_query, w_key, w_value], axis=1), ROWS, axis=0, tiled=True
    )
    wo_t = lax.all_gather(w_out.T, ROWS, axis=0, tiled=True)
    wg_full = lax.all_gather(w_gate, ROWS, axis=0, tiled=True)
    wu_full = lax.all_gather(w_up, ROWS, axis=0, tiled=True)
    wd_t = lax.all_gather(w_down.T, ROWS, axis=0, tiled=True)

    gain_sizes = (gain_attn.shape[0], gain_mlp.shape[0], gain_query.shape[0], gain_key.shape[0])
    gains = lax.all_gather(
        jnp.concatenate([gain_attn, gain_mlp, gain_query, gain_key])[None], ROWS, axis=0, tiled=True
    ).astype(F32)
    gain_parts, place = [], 0
    for size in gain_sizes:
        gain_parts.append(gains[:, place : place + size].reshape(-1))
        place += size
    gain_one, gain_two, gain_q, gain_k = gain_parts

    local = jnp.arange(row_count, dtype=jnp.int32)
    natural = ((local // chunk) ^ me_t) * chunk + local % chunk
    place_here = lax.axis_index("ctx") * row_count + natural
    place_all = (
        jnp.arange(ctx_size, dtype=jnp.int32)[:, None] * row_count + natural[None, :]
    ).reshape(-1)
    starts, reach, offset = tree_layout(lengths[0], parents[0], tree_total)
    segment_here, onehot_here = segment_onehot(place_here, starts)
    segment_all, onehot_all = segment_onehot(place_all, starts)
    position = place_here.astype(F32) + jnp.dot(
        onehot_here, offset - starts.astype(F32), precision=PRECISE
    )
    ancestor = (
        jnp.dot(jnp.dot(onehot_here, reach, precision=PRECISE), onehot_all.T, precision=PRECISE)
        > 0.5
    )
    allowed = (segment_here[:, None] == segment_all[None, :]) & (
        place_all[None, :] <= place_here[:, None]
    ) | ancestor
    half_dim = HEAD_DIM // 2
    frequency = jnp.exp(jnp.arange(half_dim, dtype=F32) * (-2.0 * math.log(THETA) / HEAD_DIM))
    angles = position[:, None] * frequency[None, :]
    cosine = jnp.cos(angles)[:, None, :]
    sine_vals = jnp.sin(angles)[:, None, :]
    score_scale = 1.0 / math.sqrt(HEAD_DIM)

    x_low = xor_order(tokens)
    g_low = xor_order(cotangent)
    inputs = x_low.astype(F32)
    scale_one = row_scales(inputs)
    normed_attn = (inputs * scale_one * gain_one).astype(BF)
    qkv = dot(normed_attn, w_qkv)
    heads_here = q_cols // HEAD_DIM
    kv_here = k_cols // HEAD_DIM
    group_size = heads_here // kv_here
    q_heads = qkv[:, :q_cols].reshape(row_count, heads_here, HEAD_DIM)
    k_heads = qkv[:, q_cols : q_cols + k_cols].reshape(row_count, kv_here, HEAD_DIM)
    v_bf = qkv[:, q_cols + k_cols :].astype(BF)
    q_scales, k_scales = row_scales(q_heads), row_scales(k_heads)
    q_bf = rotate_pairs(q_heads * q_scales * gain_q, cosine, sine_vals).astype(BF)
    k_bf = rotate_pairs(k_heads * k_scales * gain_k, cosine, sine_vals).astype(BF)
    kv_all = lax.all_gather(
        jnp.concatenate([k_bf.reshape(row_count, k_cols), v_bf], axis=1), "ctx", axis=0, tiled=True
    )
    k_all = kv_all[:, :k_cols].reshape(tree_total, kv_here, HEAD_DIM)
    v_all = kv_all[:, k_cols:].reshape(tree_total, kv_here, HEAD_DIM)
    q_grouped = q_bf.reshape(row_count, kv_here, group_size, HEAD_DIM)
    scores = (
        jnp.einsum("tkgd,skd->kgts", q_grouped, k_all, preferred_element_type=F32) * score_scale
    )
    scores = jnp.where(allowed[None, None], scores, -1e30)
    row_max = jnp.max(scores, axis=-1, keepdims=True)
    weights = jnp.exp(scores - row_max)
    prob_all = weights / jnp.sum(weights, axis=-1, keepdims=True)
    prob_bf = prob_all.astype(BF)
    mixture = jnp.einsum("kgts,skd->tkgd", prob_bf, v_all, preferred_element_type=F32)
    mixture_bf = mixture.reshape(row_count, heads_here * HEAD_DIM).astype(BF)
    own_inputs = inputs[:chunk]
    hidden = own_inputs + scatter_sum(outer_cols(mixture_bf, wo_t))

    scale_two = row_scales(hidden)
    normed_own = (hidden * scale_two * gain_two).astype(BF)
    normed_mlp = jnp.concatenate(gather_rows(normed_own), axis=0)
    gate_pre = dot(normed_mlp, wg_full)
    up_pre = dot(normed_mlp, wu_full)
    gate_sig = jax.nn.sigmoid(gate_pre)
    gate_act = gate_pre * gate_sig
    inner_bf = (gate_act * up_pre).astype(BF)

    grad_down_t = grad_scatter(g_low, inner_bf)
    grad_inner = dot(g_low, wd_t)
    grad_gate_pre = (grad_inner * up_pre * gate_sig * (1.0 + gate_pre * (1.0 - gate_sig))).astype(
        BF
    )
    grad_up_pre = (grad_inner * gate_act).astype(BF)
    grad_normed_mlp = scatter_sum(
        outer_cols(grad_gate_pre, wg_full) + outer_cols(grad_up_pre, wu_full)
    )
    grad_gate = grad_scatter(normed_mlp, grad_gate_pre)
    grad_up = grad_scatter(normed_mlp, grad_up_pre)
    own_cotangent = g_low[:chunk].astype(F32)
    grad_hidden_norm, gain_two_terms = norm_back(grad_normed_mlp, hidden, gain_two, scale_two)
    gain_two_part = jnp.sum(gain_two_terms, axis=0)
    grad_hidden = own_cotangent + grad_hidden_norm
    grad_attn_bf = jnp.concatenate(gather_rows(grad_hidden.astype(BF)), axis=0)

    result_own = (hidden + scatter_sum(outer_cols(inner_bf, wd_t))).astype(BF)
    result = xor_order(jnp.concatenate(gather_rows(result_own), axis=0))

    grad_out_t = grad_scatter(grad_attn_bf, mixture_bf)
    grad_mixture = (
        dot(grad_attn_bf, wo_t).astype(BF).reshape(row_count, kv_here, group_size, HEAD_DIM)
    )
    grad_probs = jnp.einsum("tkgd,skd->kgts", grad_mixture, v_all, preferred_element_type=F32)
    grad_v_all = jnp.einsum("kgts,tkgd->skd", prob_bf, grad_mixture, preferred_element_type=F32)
    row_total = jnp.sum(prob_all * grad_probs, axis=-1, keepdims=True)
    grad_scores = (prob_all * (grad_probs - row_total)).astype(BF)
    grad_q = (
        jnp.einsum("kgts,skd->tkgd", grad_scores, k_all, preferred_element_type=F32) * score_scale
    )
    grad_k_all = (
        jnp.einsum("kgts,tkgd->skd", grad_scores, q_grouped, preferred_element_type=F32)
        * score_scale
    )
    grad_kv = lax.psum_scatter(
        jnp.concatenate(
            [grad_k_all.reshape(tree_total, k_cols), grad_v_all.reshape(tree_total, k_cols)], axis=1
        ).astype(BF),
        "ctx",
        scatter_dimension=0,
        tiled=True,
    )
    grad_q = grad_q.reshape(row_count, heads_here, HEAD_DIM)
    grad_k = grad_kv[:, :k_cols].reshape(row_count, kv_here, HEAD_DIM).astype(F32)
    grad_v_bf = grad_kv[:, k_cols:]
    grad_q_heads, q_gain_terms = norm_back(
        rotate_back(grad_q, cosine, sine_vals), q_heads, gain_q, q_scales
    )
    grad_k_heads, k_gain_terms = norm_back(
        rotate_back(grad_k, cosine, sine_vals), k_heads, gain_k, k_scales
    )
    grad_qkv_raw = jnp.concatenate(
        [
            grad_q_heads.reshape(row_count, q_cols).astype(BF),
            grad_k_heads.reshape(row_count, k_cols).astype(BF),
            grad_v_bf,
        ],
        axis=1,
    )
    grad_qkv = grad_scatter(normed_attn, grad_qkv_raw)
    partial_back = outer_cols(grad_qkv_raw, w_qkv)
    gain_one_part = jnp.sum(partial_back * inputs * scale_one, axis=0)
    grad_normed_attn = scatter_sum(partial_back)
    grad_input_norm, unused_terms = norm_back(
        grad_normed_attn, own_inputs, gain_one, scale_one[:chunk]
    )
    grad_own = lax.optimization_barrier((grad_hidden + grad_input_norm).astype(BF))
    grad_tokens = xor_order(jnp.concatenate(gather_rows(grad_own), axis=0)).astype(F32)

    block = lax.axis_index("dp") * ctx_size + lax.axis_index("ctx")
    summed = lax.psum(
        jnp.concatenate(
            [
                gain_one_part,
                gain_two_part,
                jnp.sum(q_gain_terms, axis=(0, 1)),
                jnp.sum(k_gain_terms, axis=(0, 1)),
            ]
        ),
        ("dp", "ctx", "tensor"),
    )
    gain_grads, place = [], 0
    for size, part in zip(gain_sizes, gain_parts):
        gain_grads.append(lax.dynamic_slice_in_dim(summed, place + block * size, size))
        place += part.shape[0]

    return (
        result,
        grad_tokens,
        grad_qkv[:, :q_cols].astype(F32),
        grad_qkv[:, q_cols : q_cols + k_cols].astype(F32),
        grad_qkv[:, q_cols + k_cols :].astype(F32),
        grad_out_t.T.astype(F32),
        grad_gate.astype(F32),
        grad_up.astype(F32),
        grad_down_t.T.astype(F32),
        *gain_grads,
    )


def solution(mesh):
    rows = P(ROWS, None)
    cols = P(ROWS, "tensor")
    flipped = P("tensor", ROWS)
    vector = P(ROWS)
    return jax.shard_map(
        on_device,
        mesh=mesh,
        in_specs=(
            rows,
            P("dp", None),
            P("dp", None),
            cols,
            cols,
            cols,
            flipped,
            cols,
            cols,
            flipped,
            vector,
            vector,
            vector,
            vector,
            rows,
        ),
        out_specs=(
            rows,
            rows,
            cols,
            cols,
            cols,
            flipped,
            cols,
            cols,
            flipped,
            vector,
            vector,
            vector,
            vector,
        ),
        check_vma=False,
    )
```

time: 1470 us -> 786 us (0.53)
  waiting for transfers between devices: 1130 us -> 377 us
  local copies, waits for them, and re-layouts: 14.5 us -> 49.4 us
  starting transfers between devices: 1.31 us -> 29.5 us
    reduce_scatter x9 -> x6, waiting for transfers between devices: 540 us -> 58 us  [the longest x5 58 us: grad_scatter(): return lax.psum_scatter(both, 'ctx', scatter_dimension=0, tiled=True)]
    psum x3 -> x0, waiting for transfers between devices: 325 us -> none  [the longest x2 255 us: tensor_sum(): return lax.psum(values, 'tensor')]
    ppermute x0 -> x29, waiting for transfers between devices: none -> 140 us  [swap(): return lax.ppermute(values, axis, [(a, a ^ mask) for a in range(size)])]
    all_gather x9 -> x6, waiting for transfers between devices: 258 us -> 176 us  [the longest x1 56.3 us: on_device(): wg_full = lax.all_gather(w_gate, ROWS, axis=0, tiled=True)]
    psum x1, blocking collectives: 9.76 us -> 52.6 us  [on_device(): lax.psum(jnp.concatenate([gain_one_part, gain_two_part, jnp.sum(q_gain_te...]
    all_gather x2 -> x0, blocking collectives: 34.3 us -> none  [the longest x1 17.9 us: on_device(): lax.all_gather(gain_attn, ('dp', 'ctx'), axis=0, tiled=True)]
    ppermute x0 -> x29, starting transfers between devices: none -> 28.6 us  [swap(): return lax.ppermute(values, axis, [(a, a ^ mask) for a in range(size)])]
    dot_general x7 -> x5, matrix products: 33.5 us -> 23.9 us  [outer_cols(): lax.dot_general(left, right, (((1,), (1,)), ((), ())), preferred_element_...]
  transfers between devices with their start and end apart: 21 -> 41, of which waited for: 20 -> 27; matrix products, arithmetic and copies ran while one was open for 11% -> 23% of each run, Pallas kernels for 0% -> 0%
where the time goes in v1:
time: 786 us; the launch traced here: 779 us
  waiting for transfers between devices  377 us (48%)
  matrix products  147 us (19%)
  blocking collectives  85.9 us (11%)
  other arithmetic  73.6 us (9%)
  local copies, waits for them, and re-layouts  49.4 us (6%)
  starting transfers between devices  29.5 us (4%)
  between operations  16.5 us (2%)
    ppermute x29, waiting for transfers between devices, swap(): return lax.ppermute(values, axis, [(a, a ^ mask) for a in range(size)])  140 us
    reduce_scatter x5, waiting for transfers between devices, grad_scatter(): return lax.psum_scatter(both, 'ctx', scatter_dimension=0, tiled=True)  58 us
    all_gather x1, waiting for transfers between devices, on_device(): wg_full = lax.all_gather(w_gate, ROWS, axis=0, tiled=True)  56.3 us
    all_gather x1, waiting for transfers between devices, on_device(): wu_full = lax.all_gather(w_up, ROWS, axis=0, tiled=True)  56.3 us
    psum x1, blocking collectives, on_device(): lax.psum(jnp.concatenate([gain_one_part, gain_two_part, jnp.sum(q_gain_te...  52.6 us
    dot_general x10, matrix products, inner_rows(): lax.dot_general(left, right, (((0,), (0,)), ((), ())), preferred_element_...  35.7 us
    dot_general x5, matrix products, dot(): return jnp.dot(left, right, preferred_element_type=F32)  34.3 us
    unnamed x1, blocking collectives  33.2 us
  transfers between devices with their start and end apart: 41, of which 27 were waited for; matrix products, arithmetic and copies ran while one was open for 23% of the time, Pallas kernels for 0%

profile of v1, /device:TPU:0, one launch (start us, length us, event | category | flops | bytes accessed | tf_op | source)
XLA Modules:
  0.0 778.5 jit_solution(5190589777838731769)
XLA Ops:
  13.0 33.2 %all-reduce = bf16[4352]{0:T(1024)(128)(2,1)S(1)} all-reduce(bf16[4352]{0:T(1024)(128)(2,1)S(1)} %dynamic-update-slice), channel_id=2, replica_groups=mesh['dp'=2,'ctx'=4,'tensor'=4] {'dp','ctx'}, use_global_device_ids=true, to_apply=%add | all-reduce | flops 4352 | bytes 17408
  54.6 4.2 multiply_convert_fusion
  60.8 5.1 fusion.131
  90.4 27.5 %all-gather.10.cloned.1.call-done = bf16[2048,512]{1,0:T(8,128)(2,1)} async-done(((bf16[512,512]{1,0:T(8,128)(2,1)}), bf16[2048,512]{1,0:T(8,128)(2,1)}) %all-gather.10.cloned.1.call-update) | async-done | bytes 2097168 | tf_op jit(solution)/shard_map/all_gather | solution.py:209
  126.6 11.2 %fusion.127 = (f32[2,2,512]{2,1,0:T(2,128)S(1)}, f32[2,2,512,2048]{2,3,1,0:T(8,128)}) fusion(pred[512,2048]{0,1:T(8,128)(4,1)} %copy.47, bf16[2048,2,128,1]{0,2,3,1:T(8,128)(2,1)S(1)} %copy.71, bf16[512,2,2,64]{3,0,2,1:T(8,128)(2,1)} %bitcast.198, bf16[512,2,2,64]{3,0,2,1:T(8,128)(2,1)} %bitcast.196), kind=kOutput, calls=%fused_computation.254 | convolution fusion | flops 1091569664 | bytes 19406848 | tf_op jit(solution)/shard_map/sub | solution.py:220
  137.9 7.6 fusion.23
  145.5 3.5 all-gather.12.cloned.1.call-done
  157.5 9.4 %collective-permute-done = bf16[128,2048]{1,0:T(8,128)(2,1)S(1)} collective-permute-done((bf16[128,2048]{1,0:T(8,128)(2,1)S(1)}, bf16[128,2048]{1,0:T(8,128)(2,1)S(1)}, u32[]{:S(2)}, u32[]{:S(2)}) %collective-permute-start) | collective-permute-done | bytes 524320 | tf_op jit(solution)/shard_map/ppermute | solution.py:62
  166.8 11.5 %collective-permute-done.2 = bf16[128,2048]{1,0:T(8,128)(2,1)S(1)} collective-permute-done((bf16[128,2048]{1,0:T(8,128)(2,1)S(1)}, bf16[128,2048]{1,0:T(8,128)(2,1)S(1)}, u32[]{:S(2)}, u32[]{:S(2)}) %collective-permute-start.2) | collective-permute-done | bytes 524320 | tf_op jit(solution)/shard_map/ppermute | solution.py:62
  183.9 30.7 %all-gather.18.cloned.1.call-done = bf16[2048,1536]{0,1:T(8,128)(2,1)} async-done(((bf16[256,1536]{0,1:T(8,128)(2,1)}), bf16[2048,1536]{0,1:T(8,128)(2,1)}) %all-gather.18.cloned.1.call-update) | async-done | bytes 6291472 | tf_op jit(solution)/shard_map/all_gather | solution.py:156
  214.6 8.1 %fusion.112 = f32[512,1536]{1,0:T(8,128)} fusion(bf16[2048,1536]{0,1:T(8,128)(2,1)} %all-gather.18.cloned.1.call-done, bf16[128,2048]{1,0:T(8,128)(2,1)S(1)} %copy-done.42, bf16[128,2048]{1,0:T(8,128)(2,1)} %get-tuple-element.72, bf16[128,2048]{1,0:T(8,128)(2,1)S(1)} %copy-done.40, bf16[128,2048]{1,0:T(8,128)(2,1)S(1)} %copy-done.14), kind=kOutput, calls=%fused_computation.241 | convolution fusion | flops 3229614080 | bytes 11534336 | tf_op jit(solution)/shard_map/dot_general | solution.py:49
  222.7 56.3 %all-gather.16.cloned.1.call-done = bf16[2048,1536]{1,0:T(8,128)(2,1)} async-done(((bf16[256,1536]{1,0:T(8,128)(2,1)}), bf16[2048,1536]{1,0:T(8,128)(2,1)}) %all-gather.16.cloned.1.call-update) | async-done | bytes 6291472 | tf_op jit(solution)/shard_map/all_gather | solution.py:155
  279.0 8.5 %fusion.114 = f32[512,1536]{1,0:T(8,128)} fusion(bf16[2048,1536]{1,0:T(8,128)(2,1)} %all-gather.16.cloned.1.call-done, bf16[128,2048]{1,0:T(8,128)(2,1)} %collective-permute-done.5, bf16[128,2048]{1,0:T(8,128)(2,1)} %collective-permute-done.4, bf16[128,2048]{1,0:T(8,128)(2,1)} %collective-permute-done.3, bf16[128,2048]{1,0:T(8,128)(2,1)S(1)} %multiply_convert_fusion.4), kind=kOutput, calls=%fused_computation.243 | convolution fusion | flops 3229614080 | bytes 11534336 | tf_op jit(solution)/shard_map/dot_general | solution.py:49
  287.4 56.3 %all-gather.14.cloned.1.call-done = bf16[2048,1536]{1,0:T(8,128)(2,1)} async-done(((bf16[256,1536]{1,0:T(8,128)(2,1)}), bf16[2048,1536]{1,0:T(8,128)(2,1)}) %all-gather.14.cloned.1.call-update) | async-done | bytes 6291472 | tf_op jit(solution)/shard_map/all_gather | solution.py:154
  343.8 11.3 %multiply_convert_fusion.1 = (bf16[512,1536]{1,0:T(8,128)(2,1)S(1)}, bf16[512,1536]{1,0:T(8,128)(2,1)S(1)}, bf16[512,1536]{1,0:T(8,128)(2,1)}) fusion(f32[512,1536]{1,0:T(8,128)} %fusion.112, f32[512,1536]{1,0:T(8,128)} %fusion.114, bf16[2048,1536]{1,0:T(8,128)(2,1)} %all-gather.14.cloned.1.call-done, bf16[128,2048]{1,0:T(8,128)(2,1)} %collective-permute-done.5, ...), kind=kOutput, calls=%fused_computation.28 | convolution fusion | flops 3241410560 | bytes 19398656 | tf_op jit(solution)/shard_map/dot_general | solution.py:49
  355.2 5.1 fusion.132
  360.2 5.3 fusion.129
  369.2 11.3 %collective-permute-done.12 = bf16[128,2048]{1,0:T(8,128)(2,1)S(1)} collective-permute-done((bf16[128,2048]{1,0:T(8,128)(2,1)S(1)}, bf16[128,2048]{1,0:T(8,128)(2,1)S(1)}, u32[]{:S(2)}, u32[]{:S(2)}) %collective-permute-start.12) | collective-permute-done | bytes 524320 | tf_op jit(solution)/shard_map/ppermute | solution.py:62
  380.5 11.5 %collective-permute-done.14 = bf16[128,2048]{1,0:T(8,128)(2,1)S(1)} collective-permute-done((bf16[128,2048]{1,0:T(8,128)(2,1)S(1)}, bf16[128,2048]{1,0:T(8,128)(2,1)S(1)}, u32[]{:S(2)}, u32[]{:S(2)}) %collective-permute-start.14) | collective-permute-done | bytes 524320 | tf_op jit(solution)/shard_map/ppermute | solution.py:62
  398.0 12.2 %collective-permute-done.17 = bf16[128,2048]{1,0:T(8,128)(2,1)S(1)} collective-permute-done((bf16[128,2048]{1,0:T(8,128)(2,1)S(1)}, bf16[128,2048]{1,0:T(8,128)(2,1)S(1)}, u32[]{:S(2)}, u32[]{:S(2)}) %collective-permute-start.17) | collective-permute-done | bytes 524320 | tf_op jit(solution)/shard_map/ppermute | solution.py:62
  410.2 9.1 %collective-permute-done.16 = bf16[128,2048]{1,0:T(8,128)(2,1)S(1)} collective-permute-done((bf16[128,2048]{1,0:T(8,128)(2,1)S(1)}, bf16[128,2048]{1,0:T(8,128)(2,1)S(1)}, u32[]{:S(2)}, u32[]{:S(2)}) %collective-permute-start.16) | collective-permute-done | bytes 524320 | tf_op jit(solution)/shard_map/ppermute | solution.py:62
  420.7 9.7 %fusion.18 = bf16[2,128,2048]{2,1,0:T(8,128)(2,1)} fusion(bf16[512,2,2,128]{0,3,2,1:T(8,128)(2,1)S(1)} %bitcast.227, f32[2,2,512,2048]{2,3,1,0:T(8,128)} %get-tuple-element.115, f32[2,2,512]{2,1,0:T(2,128)S(1)} %get-tuple-element.114), kind=kOutput, calls=%fused_computation.38 | convolution fusion | flops 1082654720 | bytes 18358272 | tf_op jit(solution)/shard_map/kgts,tkgd->skd/dot_general | solution.py:262
  430.4 10.7 %fusion.1 = (f32[2,2,512]{2,1,0:T(2,128)S(1)}, f32[2,2048,512,2]{2,1,3,0:T(8,128)}) fusion(f32[2,2,512,2048]{2,3,1,0:T(8,128)} %get-tuple-element.115, f32[2,2,512]{2,1,0:T(2,128)S(1)} %get-tuple-element.114, bf16[512,2,2,128]{0,3,2,1:T(8,128)(2,1)S(1)} %bitcast.228, bf16[2048,2,128,1]{2,1,0,3:T(2,128)(2,1)S(1)} %bitcast.205), kind=kOutput, calls=%fused_computation.3 | convolution fusion | flops 1086322688 | bytes 35143680 | tf_op jit(solution)/shard_map/tkgd,skd->kgts/dot_general | solution.py:261
  443.3 11.8 %fusion.3 = bf16[2,2,512,2048]{2,3,1,0:T(8,128)(2,1)S(1)} fusion(f32[2,2048,512,2]{2,1,3,0:T(8,128)} %get-tuple-element.121, f32[2,2,512]{2,1,0:T(2,128)S(1)} %get-tuple-element.120, f32[2,2,512,2048]{2,3,1,0:T(8,128)} %get-tuple-element.115, f32[2,2,512]{2,1,0:T(2,128)S(1)} %get-tuple-element.114), kind=kLoop, calls=%fused_computation.5 | loop fusion | flops 16777216 | bytes 41959424 | tf_op jit(solution)/shard_map/convert_element_type | solution.py:264
  455.2 3.7 fusion.17
  461.2 3.1 pad_maximum_fusion.6
  466.1 3.6 convolution_convert_fusion
  473.6 3.6 collective-permute-done.25
  477.2 3.3 add_convert_fusion.4
  480.6 6.2 add_convert_fusion
  491.8 5.5 collective-permute-done.26
  497.3 3.5 add_convert_fusion.2
  501.1 5.2 convolution_convert_fusion.1
  506.5 5.8 collective-permute-done.27
  512.4 6.4 add_convert_fusion.1
  520.0 4.7 convolution_multiply_fusion
  546.5 5.3 fusion.130
  551.8 5.3 multiply_reduce_fusion
  567.7 5.6 collective-permute-done.18
  573.9 10.8 %collective-permute-done.20 = bf16[128,2048]{1,0:T(8,128)(2,1)} collective-permute-done((bf16[128,2048]{1,0:T(8,128)(2,1)}, bf16[128,2048]{1,0:T(8,128)(2,1)}, u32[]{:S(2)}, u32[]{:S(2)}) %collective-permute-start.20) | collective-permute-done | bytes 524320 | tf_op jit(solution)/shard_map/ppermute | solution.py:62
  589.0 7.0 collective-permute-done.6
  596.0 10.5 %collective-permute-done.8 = bf16[128,2048]{1,0:T(8,128)(2,1)} collective-permute-done((bf16[128,2048]{1,0:T(8,128)(2,1)}, bf16[128,2048]{1,0:T(8,128)(2,1)}, u32[]{:S(2)}, u32[]{:S(2)}) %collective-permute-start.8) | collective-permute-done | bytes 524320 | tf_op jit(solution)/shard_map/ppermute | solution.py:62
  607.7 4.7 add_convert_fusion.5
  618.0 52.6 %psum.7 = f32[4352]{0:T(1024)S(1)} all-reduce(f32[4352]{0:T(1024)S(1)} %pad_maximum_fusion.15), channel_id=1, replica_groups=mesh['dp'=2,'ctx'=4,'tensor'=4] {'dp','ctx','tensor'}, use_global_device_ids=true, to_apply=%region_26.27 | all-reduce | flops 4352 | bytes 34816 | tf_op jit(solution)/shard_map/psum | solution.py:308
  677.1 10.7 %collective-permute-done.11 = bf16[128,2048]{1,0:T(8,128)(2,1)S(1)} collective-permute-done((bf16[128,2048]{1,0:T(8,128)(2,1)}, bf16[128,2048]{1,0:T(8,128)(2,1)S(1)}, u32[]{:S(2)}, u32[]{:S(2)}) %collective-permute-start.11) | collective-permute-done | bytes 524320 | tf_op jit(solution)/shard_map/ppermute | solution.py:62
  687.8 9.3 %collective-permute-done.10 = bf16[128,2048]{1,0:T(8,128)(2,1)S(1)} collective-permute-done((bf16[128,2048]{1,0:T(8,128)(2,1)}, bf16[128,2048]{1,0:T(8,128)(2,1)S(1)}, u32[]{:S(2)}, u32[]{:S(2)}) %collective-permute-start.10) | collective-permute-done | bytes 524320 | tf_op jit(solution)/shard_map/ppermute | solution.py:62
  707.1 14.8 %reduce-scatter.15.cloned.1.call-done = bf16[256,1536]{1,0:T(8,128)(2,1)} async-done(((bf16[1024,1536]{1,0:T(8,128)(2,1)}), bf16[256,1536]{1,0:T(8,128)(2,1)}) %reduce-scatter.15.cloned.1.call-update) | async-done | bytes 786448 | tf_op jit(solution)/shard_map/reduce_scatter | solution.py:100
  724.4 43.3 %reduce-scatter.9.cloned.1.call-done = bf16[256,1024]{1,0:T(8,128)(2,1)} async-done(((bf16[1024,1024]{1,0:T(8,128)(2,1)}), bf16[256,1024]{1,0:T(8,128)(2,1)}) %reduce-scatter.9.cloned.1.call-update) | async-done | bytes 524304 | tf_op jit(solution)/shard_map/reduce_scatter | solution.py:100
  (344 shorter events, 156.3 us)
Async XLA Ops:
  7.2 53.6 %all-gather.8.cloned.1.call-start = ((), (), s32[]{:S(2)}) async-start(), calls=%async_computation.6 | async-start | bytes 4718592 | tf_op jit(solution)/shard_map/all_gather | solution.py:150
  9.2 108.7 %all-gather.10.cloned.1.call-start = ((), (), s32[]{:S(2)}) async-start(), calls=%async_computation.7 | async-start | bytes 2621440 | tf_op jit(solution)/shard_map/all_gather | solution.py:209
  52.2 104.7 %copy-start.6 = (bf16[128,2048]{1,0:T(8,128)(2,1)}, bf16[128,2048]{1,0:T(8,128)(2,1)S(1)}, u32[]{:S(2)}) copy-start(bf16[128,2048]{1,0:T(8,128)(2,1)S(1)} %get-tuple-element.85) | copy-start | bytes 1572868
  52.2 104.7 %copy-start.8 = (bf16[128,2048]{1,0:T(8,128)(2,1)}, bf16[128,2048]{1,0:T(8,128)(2,1)S(1)}, u32[]{:S(2)}) copy-start(bf16[128,2048]{1,0:T(8,128)(2,1)S(1)} %get-tuple-element.86) | copy-start | bytes 1572868
  52.3 104.7 %copy-start.10 = (bf16[128,2048]{1,0:T(8,128)(2,1)}, bf16[128,2048]{1,0:T(8,128)(2,1)S(1)}, u32[]{:S(2)}) copy-start(bf16[128,2048]{1,0:T(8,128)(2,1)S(1)} %get-tuple-element.87) | copy-start | bytes 1572868
  52.3 104.7 %copy-start.12 = (bf16[128,2048]{1,0:T(8,128)(2,1)}, bf16[128,2048]{1,0:T(8,128)(2,1)S(1)}, u32[]{:S(2)}) copy-start(bf16[128,2048]{1,0:T(8,128)(2,1)S(1)} %get-tuple-element.88) | copy-start | bytes 1572868
  73.2 75.7 %all-gather.12.cloned.1.call-start = ((), (), s32[]{:S(2)}) async-start(), calls=%async_computation.8 | async-start | bytes 2359296 | tf_op jit(solution)/shard_map/all_gather | solution.py:153
  74.0 140.6 %all-gather.18.cloned.1.call-start = ((), (), s32[]{:S(2)}) async-start(), calls=%async_computation.11 | async-start | bytes 7077888 | tf_op jit(solution)/shard_map/all_gather | solution.py:156
  74.5 204.4 %all-gather.16.cloned.1.call-start = ((), (), s32[]{:S(2)}) async-start(), calls=%async_computation.10 | async-start | bytes 7077888 | tf_op jit(solution)/shard_map/all_gather | solution.py:155
  75.1 268.7 %all-gather.14.cloned.1.call-start = ((), (), s32[]{:S(2)}) async-start(), calls=%async_computation.9 | async-start | bytes 7077888 | tf_op jit(solution)/shard_map/all_gather | solution.py:154
  75.7 459.8 %reduce-scatter.7.cloned.1.call-start = ((), (), s32[]{:S(2)}) async-start(), calls=%async_computation.12 | async-start | bytes 2621440 | tf_op jit(solution)/shard_map/reduce_scatter | solution.py:272
  152.0 14.9 %collective-permute-start = (bf16[128,2048]{1,0:T(8,128)(2,1)S(1)}, bf16[128,2048]{1,0:T(8,128)(2,1)S(1)}, u32[]{:S(2)}, u32[]{:S(2)}) collective-permute-start(bf16[128,2048]{1,0:T(8,128)(2,1)S(1)} %get-tuple-element.80), channel_id=1, source_target_pairs={{0,1},{1,0},{2,3},{3,2},{4,5},{5,4},{6,7},{7,6},{8,9},{9,8},{10,11... | collective-permute-start | bytes 1572872 | tf_op jit(solution)/shard_map/ppermute | solution.py:62
  153.4 24.8 %collective-permute-start.2 = (bf16[128,2048]{1,0:T(8,128)(2,1)S(1)}, bf16[128,2048]{1,0:T(8,128)(2,1)S(1)}, u32[]{:S(2)}, u32[]{:S(2)}) collective-permute-start(bf16[128,2048]{1,0:T(8,128)(2,1)S(1)} %get-tuple-element.81), channel_id=1, source_target_pairs={{0,3},{1,2},{2,1},{3,0},{4,7},{5,6},{6,5},{7,4},{8,11},{9,10},{10,... | collective-permute-start | bytes 1572872 | tf_op jit(solution)/shard_map/ppermute | solution.py:62
  154.9 24.7 %collective-permute-start.1 = (bf16[128,2048]{1,0:T(8,128)(2,1)S(1)}, bf16[128,2048]{1,0:T(8,128)(2,1)S(1)}, u32[]{:S(2)}, u32[]{:S(2)}) collective-permute-start(bf16[128,2048]{1,0:T(8,128)(2,1)S(1)} %get-tuple-element.82), channel_id=1, source_target_pairs={{0,2},{1,3},{2,0},{3,1},{4,6},{5,7},{6,4},{7,5},{8,10},{9,11},{10,... | collective-permute-start | bytes 1572872 | tf_op jit(solution)/shard_map/ppermute | solution.py:62
  180.3 163.5 %copy-start.36 = (bf16[128,2048]{1,0:T(8,128)(2,1)}, bf16[128,2048]{1,0:T(8,128)(2,1)S(1)}, u32[]{:S(2)}) copy-start(bf16[128,2048]{1,0:T(8,128)(2,1)S(1)} %multiply_convert_fusion.4) | copy-start | bytes 1572868
  180.3 98.7 %collective-permute-start.5 = (bf16[128,2048]{1,0:T(8,128)(2,1)S(1)}, bf16[128,2048]{1,0:T(8,128)(2,1)}, u32[]{:S(2)}, u32[]{:S(2)}) collective-permute-start(bf16[128,2048]{1,0:T(8,128)(2,1)S(1)} %multiply_convert_fusion.4), channel_id=1, source_target_pairs={{0,3},{1,2},{2,1},{3,0},{4,7},{5,6},{6,5},{7,4},{8,11},{9,10},{10,... | collective-permute-start | bytes 1572872 | tf_op jit(solution)/shard_map/ppermute | solution.py:62
  181.8 97.1 %collective-permute-start.4 = (bf16[128,2048]{1,0:T(8,128)(2,1)S(1)}, bf16[128,2048]{1,0:T(8,128)(2,1)}, u32[]{:S(2)}, u32[]{:S(2)}) collective-permute-start(bf16[128,2048]{1,0:T(8,128)(2,1)S(1)} %multiply_convert_fusion.4), channel_id=1, source_target_pairs={{0,2},{1,3},{2,0},{3,1},{4,6},{5,7},{6,4},{7,5},{8,10},{9,11},{10,... | collective-permute-start | bytes 1572872 | tf_op jit(solution)/shard_map/ppermute | solution.py:62
  183.3 95.7 %collective-permute-start.3 = (bf16[128,2048]{1,0:T(8,128)(2,1)S(1)}, bf16[128,2048]{1,0:T(8,128)(2,1)}, u32[]{:S(2)}, u32[]{:S(2)}) collective-permute-start(bf16[128,2048]{1,0:T(8,128)(2,1)S(1)} %multiply_convert_fusion.4), channel_id=1, source_target_pairs={{0,1},{1,0},{2,3},{3,2},{4,5},{5,4},{6,7},{7,6},{8,9},{9,8},{10,11... | collective-permute-start | bytes 1572872 | tf_op jit(solution)/shard_map/ppermute | solution.py:62
  365.7 14.9 %collective-permute-start.12 = (bf16[128,2048]{1,0:T(8,128)(2,1)S(1)}, bf16[128,2048]{1,0:T(8,128)(2,1)S(1)}, u32[]{:S(2)}, u32[]{:S(2)}) collective-permute-start(bf16[128,2048]{1,0:T(8,128)(2,1)S(1)} %get-tuple-element.66), channel_id=1, source_target_pairs={{0,1},{1,0},{2,3},{3,2},{4,5},{5,4},{6,7},{7,6},{8,9},{9,8},{10,11... | collective-permute-start | bytes 1572872 | tf_op jit(solution)/shard_map/ppermute | solution.py:62
  367.2 24.8 %collective-permute-start.14 = (bf16[128,2048]{1,0:T(8,128)(2,1)S(1)}, bf16[128,2048]{1,0:T(8,128)(2,1)S(1)}, u32[]{:S(2)}, u32[]{:S(2)}) collective-permute-start(bf16[128,2048]{1,0:T(8,128)(2,1)S(1)} %get-tuple-element.67), channel_id=1, source_target_pairs={{0,3},{1,2},{2,1},{3,0},{4,7},{5,6},{6,5},{7,4},{8,11},{9,10},{10,... | collective-permute-start | bytes 1572872 | tf_op jit(solution)/shard_map/ppermute | solution.py:62
  368.7 24.7 %collective-permute-start.13 = (bf16[128,2048]{1,0:T(8,128)(2,1)S(1)}, bf16[128,2048]{1,0:T(8,128)(2,1)S(1)}, u32[]{:S(2)}, u32[]{:S(2)}) collective-permute-start(bf16[128,2048]{1,0:T(8,128)(2,1)S(1)} %get-tuple-element.68), channel_id=1, source_target_pairs={{0,2},{1,3},{2,0},{3,1},{4,6},{5,7},{6,4},{7,5},{8,10},{9,11},{10,... | collective-permute-start | bytes 1572872 | tf_op jit(solution)/shard_map/ppermute | solution.py:62
  394.4 15.8 %collective-permute-start.17 = (bf16[128,2048]{1,0:T(8,128)(2,1)S(1)}, bf16[128,2048]{1,0:T(8,128)(2,1)S(1)}, u32[]{:S(2)}, u32[]{:S(2)}) collective-permute-start(bf16[128,2048]{1,0:T(8,128)(2,1)S(1)} %fusion.111), channel_id=1, source_target_pairs={{0,3},{1,2},{2,1},{3,0},{4,7},{5,6},{6,5},{7,4},{8,11},{9,10},{10,... | collective-permute-start | bytes 1572872 | tf_op jit(solution)/shard_map/ppermute | solution.py:62
  396.0 23.3 %collective-permute-start.16 = (bf16[128,2048]{1,0:T(8,128)(2,1)S(1)}, bf16[128,2048]{1,0:T(8,128)(2,1)S(1)}, u32[]{:S(2)}, u32[]{:S(2)}) collective-permute-start(bf16[128,2048]{1,0:T(8,128)(2,1)S(1)} %fusion.111), channel_id=1, source_target_pairs={{0,2},{1,3},{2,0},{3,1},{4,6},{5,7},{6,4},{7,5},{8,10},{9,11},{10,... | collective-permute-start | bytes 1572872 | tf_op jit(solution)/shard_map/ppermute | solution.py:62
  397.4 21.9 %collective-permute-start.15 = (bf16[128,2048]{1,0:T(8,128)(2,1)S(1)}, bf16[128,2048]{1,0:T(8,128)(2,1)S(1)}, u32[]{:S(2)}, u32[]{:S(2)}) collective-permute-start(bf16[128,2048]{1,0:T(8,128)(2,1)S(1)} %fusion.111), channel_id=1, source_target_pairs={{0,1},{1,0},{2,3},{3,2},{4,5},{5,4},{6,7},{7,6},{8,9},{9,8},{10,11... | collective-permute-start | bytes 1572872 | tf_op jit(solution)/shard_map/ppermute | solution.py:62
  464.3 151.7 %reduce-scatter.11.cloned.1.call-start = ((), (), s32[]{:S(2)}) async-start(), calls=%async_computation.14 | async-start | bytes 1310720 | tf_op jit(solution)/shard_map/reduce_scatter | solution.py:100
  469.7 10.9 %collective-permute-start.28 = (bf16[1024,1536]{1,0:T(8,128)(2,1)}, bf16[1024,1536]{1,0:T(8,128)(2,1)}, u32[]{:S(2)}, u32[]{:S(2)}) collective-permute-start(bf16[1024,1536]{1,0:T(8,128)(2,1)} %convolution_convert_fusion), channel_id=1, source_target_pairs={{0,16},{16,0},{1,17},{17,1},{2,18},{18,2},{3,19},{19,3},{4,20},{20... | collective-permute-start | bytes 9437192 | tf_op jit(solution)/shard_map/ppermute | solution.py:62
  473.1 4.1 collective-permute-start.25
  480.5 221.2 %reduce-scatter.17.cloned.1.call-start = ((), (), s32[]{:S(2)}) async-start(), calls=%async_computation.17 | async-start | bytes 3932160 | tf_op jit(solution)/shard_map/reduce_scatter | solution.py:100
  486.8 217.8 %reduce-scatter.13.cloned.1.call-start = ((), (), s32[]{:S(2)}) async-start(), calls=%async_computation.15 | async-start | bytes 3932160 | tf_op jit(solution)/shard_map/reduce_scatter | solution.py:100
  491.6 5.7 collective-permute-start.26
  500.9 221.0 %reduce-scatter.15.cloned.1.call-start = ((), (), s32[]{:S(2)}) async-start(), calls=%async_computation.16 | async-start | bytes 3932160 | tf_op jit(solution)/shard_map/reduce_scatter | solution.py:100
  506.4 6.0 collective-permute-start.27
  518.7 248.9 %reduce-scatter.9.cloned.1.call-start = ((), (), s32[]{:S(2)}) async-start(), calls=%async_computation.13 | async-start | bytes 2621440 | tf_op jit(solution)/shard_map/reduce_scatter | solution.py:100
  545.8 18.1 %collective-permute-start.24 = (bf16[1024,1024]{1,0:T(8,128)(2,1)S(1)}, bf16[1024,1024]{1,0:T(8,128)(2,1)S(1)}, u32[]{:S(2)}, u32[]{:S(2)}) collective-permute-start(bf16[1024,1024]{1,0:T(8,128)(2,1)S(1)} %convolution_convert_fusion.3), channel_id=1, source_target_pairs={{0,16},{16,0},{1,17},{17,1},{2,18},{18,2},{3,19},{19,3},{4,20},{20... | collective-permute-start | bytes 6291464 | tf_op jit(solution)/shard_map/ppermute | solution.py:62
  558.4 15.0 %collective-permute-start.18 = (bf16[128,2048]{1,0:T(8,128)(2,1)}, bf16[128,2048]{1,0:T(8,128)(2,1)S(1)}, u32[]{:S(2)}, u32[]{:S(2)}) collective-permute-start(bf16[128,2048]{1,0:T(8,128)(2,1)} %get-tuple-element.63), channel_id=1, source_target_pairs={{0,1},{1,0},{2,3},{3,2},{4,5},{5,4},{6,7},{7,6},{8,9},{9,8},{10,11... | collective-permute-start | bytes 1572872 | tf_op jit(solution)/shard_map/ppermute | solution.py:62
  559.2 25.5 %collective-permute-start.20 = (bf16[128,2048]{1,0:T(8,128)(2,1)}, bf16[128,2048]{1,0:T(8,128)(2,1)}, u32[]{:S(2)}, u32[]{:S(2)}) collective-permute-start(bf16[128,2048]{1,0:T(8,128)(2,1)} %get-tuple-element.64), channel_id=1, source_target_pairs={{0,3},{1,2},{2,1},{3,0},{4,7},{5,6},{6,5},{7,4},{8,11},{9,10},{10,... | collective-permute-start | bytes 1572872 | tf_op jit(solution)/shard_map/ppermute | solution.py:62
  560.4 26.3 %collective-permute-start.19 = (bf16[128,2048]{1,0:T(8,128)(2,1)}, bf16[128,2048]{1,0:T(8,128)(2,1)}, u32[]{:S(2)}, u32[]{:S(2)}) collective-permute-start(bf16[128,2048]{1,0:T(8,128)(2,1)} %get-tuple-element.65), channel_id=1, source_target_pairs={{0,2},{1,3},{2,0},{3,1},{4,6},{5,7},{6,4},{7,5},{8,10},{9,11},{10,... | collective-permute-start | bytes 1572872 | tf_op jit(solution)/shard_map/ppermute | solution.py:62
  563.0 33.0 %collective-permute-start.6 = (bf16[128,2048]{1,0:T(8,128)(2,1)}, bf16[128,2048]{1,0:T(8,128)(2,1)}, u32[]{:S(2)}, u32[]{:S(2)}) collective-permute-start(bf16[128,2048]{1,0:T(8,128)(2,1)} %get-tuple-element.77), channel_id=1, source_target_pairs={{0,1},{1,0},{2,3},{3,2},{4,5},{5,4},{6,7},{7,6},{8,9},{9,8},{10,11... | collective-permute-start | bytes 1572872 | tf_op jit(solution)/shard_map/ppermute | solution.py:62
  563.9 42.7 %collective-permute-start.8 = (bf16[128,2048]{1,0:T(8,128)(2,1)}, bf16[128,2048]{1,0:T(8,128)(2,1)}, u32[]{:S(2)}, u32[]{:S(2)}) collective-permute-start(bf16[128,2048]{1,0:T(8,128)(2,1)} %get-tuple-element.78), channel_id=1, source_target_pairs={{0,3},{1,2},{2,1},{3,0},{4,7},{5,6},{6,5},{7,4},{8,11},{9,10},{10,... | collective-permute-start | bytes 1572872 | tf_op jit(solution)/shard_map/ppermute | solution.py:62
  567.7 40.0 %copy-start.15 = (bf16[128,2048]{1,0:T(8,128)(2,1)S(1)}, bf16[128,2048]{1,0:T(8,128)(2,1)}, u32[]{:S(2)}) copy-start(bf16[128,2048]{1,0:T(8,128)(2,1)} %get-tuple-element.69) | copy-start | bytes 1572868
  567.7 40.0 %slice-start = ((f32[512]{0:T(512)}), f32[128]{0:T(128)S(1)}, s32[]{:S(2)}) async-start(f32[512]{0:T(512)} %copy-done.59), calls=%async_computation.18 | async-start | bytes 1024 | tf_op jit(solution)/shard_map/slice | solution.py:302
  573.4 34.4 %collective-permute-start.7 = (bf16[128,2048]{1,0:T(8,128)(2,1)}, bf16[128,2048]{1,0:T(8,128)(2,1)S(1)}, u32[]{:S(2)}, u32[]{:S(2)}) collective-permute-start(bf16[128,2048]{1,0:T(8,128)(2,1)} %get-tuple-element.79), channel_id=1, source_target_pairs={{0,2},{1,3},{2,0},{3,1},{4,6},{5,7},{6,4},{7,5},{8,10},{9,11},{10,... | collective-permute-start | bytes 1572872 | tf_op jit(solution)/shard_map/ppermute | solution.py:62
  612.5 63.1 %collective-permute-start.23 = (bf16[128,2048]{1,0:T(8,128)(2,1)}, bf16[128,2048]{1,0:T(8,128)(2,1)S(1)}, u32[]{:S(2)}, u32[]{:S(2)}) collective-permute-start(bf16[128,2048]{1,0:T(8,128)(2,1)} %get-tuple-element.91), channel_id=1, source_target_pairs={{0,3},{1,2},{2,1},{3,0},{4,7},{5,6},{6,5},{7,4},{8,11},{9,10},{10,... | collective-permute-start | bytes 1572872 | tf_op jit(solution)/shard_map/ppermute | solution.py:62
  614.2 61.4 %collective-permute-start.22 = (bf16[128,2048]{1,0:T(8,128)(2,1)}, bf16[128,2048]{1,0:T(8,128)(2,1)S(1)}, u32[]{:S(2)}, u32[]{:S(2)}) collective-permute-start(bf16[128,2048]{1,0:T(8,128)(2,1)} %get-tuple-element.91), channel_id=1, source_target_pairs={{0,2},{1,3},{2,0},{3,1},{4,6},{5,7},{6,4},{7,5},{8,10},{9,11},{10,... | collective-permute-start | bytes 1572872 | tf_op jit(solution)/shard_map/ppermute | solution.py:62
  615.4 60.2 %collective-permute-start.21 = (bf16[128,2048]{1,0:T(8,128)(2,1)}, bf16[128,2048]{1,0:T(8,128)(2,1)S(1)}, u32[]{:S(2)}, u32[]{:S(2)}) collective-permute-start(bf16[128,2048]{1,0:T(8,128)(2,1)} %get-tuple-element.91), channel_id=1, source_target_pairs={{0,1},{1,0},{2,3},{3,2},{4,5},{5,4},{6,7},{7,6},{8,9},{9,8},{10,11... | collective-permute-start | bytes 1572872 | tf_op jit(solution)/shard_map/ppermute | solution.py:62
  671.8 15.9 %collective-permute-start.11 = (bf16[128,2048]{1,0:T(8,128)(2,1)}, bf16[128,2048]{1,0:T(8,128)(2,1)S(1)}, u32[]{:S(2)}, u32[]{:S(2)}) collective-permute-start(bf16[128,2048]{1,0:T(8,128)(2,1)} %get-tuple-element.92), channel_id=1, source_target_pairs={{0,3},{1,2},{2,1},{3,0},{4,7},{5,6},{6,5},{7,4},{8,11},{9,10},{10,... | collective-permute-start | bytes 1572872 | tf_op jit(solution)/shard_map/ppermute | solution.py:62
  674.1 23.0 %collective-permute-start.10 = (bf16[128,2048]{1,0:T(8,128)(2,1)}, bf16[128,2048]{1,0:T(8,128)(2,1)S(1)}, u32[]{:S(2)}, u32[]{:S(2)}) collective-permute-start(bf16[128,2048]{1,0:T(8,128)(2,1)} %get-tuple-element.92), channel_id=1, source_target_pairs={{0,2},{1,3},{2,0},{3,1},{4,6},{5,7},{6,4},{7,5},{8,10},{9,11},{10,... | collective-permute-start | bytes 1572872 | tf_op jit(solution)/shard_map/ppermute | solution.py:62
  675.6 21.5 %collective-permute-start.9 = (bf16[128,2048]{1,0:T(8,128)(2,1)}, bf16[128,2048]{1,0:T(8,128)(2,1)S(1)}, u32[]{:S(2)}, u32[]{:S(2)}) collective-permute-start(bf16[128,2048]{1,0:T(8,128)(2,1)} %get-tuple-element.92), channel_id=1, source_target_pairs={{0,1},{1,0},{2,3},{3,2},{4,5},{5,4},{6,7},{7,6},{8,9},{9,8},{10,11... | collective-permute-start | bytes 1572872 | tf_op jit(solution)/shard_map/ppermute | solution.py:62
  (67 other events, 556.2 us)
Sparse Core Ops, SparseCore 0:
  10.2 50.5 all-gather.7
  73.3 44.5 all-gather.9
  119.5 29.4 all-gather.11
  150.4 64.1 all-gather.17
  216.0 62.8 all-gather.15
  280.4 63.3 all-gather.13
  464.4 41.3 reduce-scatter.6
  508.1 26.4 reduce-scatter.10
  536.9 58.9 reduce-scatter.16
  598.0 61.0 reduce-scatter.12
  661.4 60.4 reduce-scatter.14
  724.1 43.5 reduce-scatter.8
